TPU v7x, 32 devices: a whole 2x2x4 slice. The times are simulated.
32 devices in a mesh: ja: 8 (over z, y), pt: 4 (over x, core).
Axes of the slice: x: 2, y: 2, z: 4, core: 2. Of those that a mesh axis runs over, the one named last changes fastest.
Arguments:
- amplitudes: bfloat16 [8, 4, 3072, 512], P('ja', 'pt'), may hold values from -6 to 6
- live_rows: int32 [8, 4], P('ja', 'pt'), may hold values from 384 to 3072, as said below
- hole_coupling: bfloat16 [8, 4, 3, 512, 512], P('ja', 'pt'), may hold values from -0.25 to 0.25
- part_hole: bfloat16 [8, 4, 3072, 512], P('ja', 'pt'), may hold values from -0.0048828125 to 0.0048828125
- recoupling: float32 [8, 3], replicated, may hold values from -1 to 1
Outputs:
- operator_bar: bfloat16 [8, 4, 3072, 512], P('ja', 'pt')
Inputs may be any that keep to these rules, and one draw needn't show every extreme that they name: `live_rows`: rows in use of a channel; some channel has exactly 3072.
All inputs are finite; a program needn't handle non-finite values.
Results may differ from a plain program's by a relative error of at most 0.0085.
Values may be sent and summed in bfloat16 or wider, within the bound.
A program may use at most 128 MiB of HBM per device.

v0:
```python
import jax
import jax.numpy as jnp
from jax import lax
from jax.sharding import PartitionSpec as P


def partner_2(block, axis, bit):
    count = lax.axis_size(axis)
    route = []
    for low in range(count):
        high = low | 1 << bit
        if high != low and high < count:
            route += [(low, high), (high, low)]
    return lax.ppermute(block, axis, route)


def with_halo(cells, sides, width):
    for axis, dim in sides:
        count = lax.axis_size(axis)
        ends = count - 1
        head = lax.slice_in_dim(cells, 0, width, axis=dim)
        tail = lax.slice_in_dim(cells, cells.shape[dim] - width, cells.shape[dim], axis=dim)
        cells = jnp.concatenate(
            [
                lax.ppermute(tail, axis, [(i, (i + 1) % count) for i in range(ends)]),
                cells,
                lax.ppermute(head, axis, [((i + 1) % count, i) for i in range(ends)]),
            ],
            axis=dim,
        )
    return cells


def segment_weights(recoupling):
    chan_total = recoupling.shape[0]
    half_count = chan_total // 2
    position = jnp.arange(chan_total, dtype=jnp.int32) % half_count
    keep = jnp.stack([position > 0, position >= 0, position < half_count - 1], axis=1)
    return jnp.where(keep, recoupling, jnp.zeros((), recoupling.dtype))


def shards(amplitudes, live_rows, hole_coupling, part_hole, recoupling):
    chan_count = amplitudes.shape[0]
    row_count = amplitudes.shape[2]
    hole_count = amplitudes.shape[3]
    first_chan = lax.axis_index("ja") * chan_count
    row_ids = lax.broadcasted_iota(jnp.int32, (chan_count, row_count), 1)
    live_mask = row_ids < live_rows[:, 0][:, None]
    masked = jnp.where(live_mask[:, :, None], amplitudes[:, 0], jnp.zeros((), jnp.bfloat16))
    inter_hh = jnp.einsum(
        "jph,jpk->jhk", masked, part_hole[:, 0], preferred_element_type=jnp.float32
    ).astype(jnp.bfloat16)
    padded_recoup = jnp.pad(segment_weights(recoupling), ((1, 1), (0, 0)))
    stacked = jnp.concatenate(
        [masked, hole_coupling[:, 0].reshape(chan_count, 3 * hole_count, hole_count), inter_hh],
        axis=1,
    )
    partner = partner_2(stacked, "pt", 1)
    extended = with_halo(partner, (("ja", 0),), 1)
    weights = lax.dynamic_slice_in_dim(padded_recoup, first_chan, chan_count + 2, 0)
    term_sum = jnp.zeros((chan_count, row_count, hole_count), jnp.float32)
    mixing = jnp.zeros((chan_count, hole_count, hole_count), jnp.float32)
    for offset in range(3):
        out_slot = 2 - offset
        source = extended[offset : offset + chan_count]
        factor = weights[offset : offset + chan_count, out_slot][:, None, None]
        hole_block = source[
            :, row_count + out_slot * hole_count : row_count + (out_slot + 1) * hole_count
        ]
        term_sum = term_sum + factor * jnp.einsum(
            "jph,jhk->jpk", source[:, :row_count], hole_block, preferred_element_type=jnp.float32
        )
        mixing = mixing + factor * source[:, row_count + 3 * hole_count :].astype(jnp.float32)
    mix_bf = mixing.astype(jnp.bfloat16)
    term_sum = term_sum + jnp.einsum(
        "jph,jhk->jpk", masked, mix_bf, preferred_element_type=jnp.float32
    )
    result = jnp.where(live_mask[:, :, None], term_sum, jnp.zeros((), jnp.float32)).astype(
        jnp.bfloat16
    )
    return result[:, None]


def solution(mesh):
    in_specs = (
        P("ja", "pt", None, None),
        P("ja", "pt"),
        P("ja", "pt", None, None, None),
        P("ja", "pt", None, None),
        P(),
    )
    out_specs = P("ja", "pt", None, None)
    return jax.shard_map(shards, mesh=mesh, in_specs=in_specs, out_specs=out_specs, check_vma=False)
```

profile of v0, /device:TPU:0, one launch (start us, length us, event | category | flops | bytes accessed | tf_op | source)
XLA Modules:
  0.0 381.8 jit_solution(8851589888757590305)
XLA Ops:
  0.0 0.0 copy-start
  0.0 0.0 copy-start.1
  0.8 3.4 bitcast_select_fusion.1
  4.2 0.0 copy-done
  4.2 0.0 copy-done.1
  4.2 0.0 copy-start.3
  4.3 2.0 fusion.13
  6.2 0.0 copy-done.3
  6.2 0.0 copy-start.4
  6.2 15.1 %pad_maximum_fusion = bf16[1,5120,512]{2,1,0:T(8,128)(2,1)} fusion(bf16[1,512,512]{2,1,0:T(8,128)(2,1)S(1)} %fusion.13, bf16[1,1536,512]{2,1,0:T(8,128)(2,1)S(1)} %bitcast.61, bf16[1,3072,512]{2,1,0:T(8,128)(2,1)S(1)} %bitcast_select_fusion.1), kind=kLoop, calls=%fused_computation.1 | loop fusion | flops 15728640 | bytes 10485760 | tf_op jit(solution)/shard_map/concatenate | solution.py:54
  21.3 3.0 collective-permute-start
  24.3 113.4 %collective-permute-done = bf16[1,5120,512]{2,1,0:T(8,128)(2,1)} collective-permute-done((bf16[1,5120,512]{2,1,0:T(8,128)(2,1)}, bf16[1,5120,512]{2,1,0:T(8,128)(2,1)}, u32[]{:S(2)}, u32[]{:S(2)}) %collective-permute-start) | collective-permute-done | bytes 5242912 | tf_op jit(solution)/shard_map/ppermute | solution.py:14
  137.6 6.0 %collective-permute-start.1 = (bf16[1,5120,512]{2,1,0:T(8,128)(2,1)}, bf16[1,5120,512]{2,1,0:T(8,128)(2,1)}, u32[]{:S(2)}, u32[]{:S(2)}) collective-permute-start(bf16[1,5120,512]{2,1,0:T(8,128)(2,1)} %collective-permute-done), channel_id=1, source_target_pairs={{0,4},{4,8},{8,12},{12,16},{16,20},{20,24},{24,28},{1,5},{5,9},{9,... | collective-permute-start | bytes 15728648 | tf_op jit(solution)/shard_map/ppermute | solution.py:25
  143.7 1.5 collective-permute-start.2
  145.2 0.0 copy-done.4
  145.2 0.1 pad_dynamic-slice_fusion
  145.3 0.6 fusion.28
  145.9 3.8 fusion.1
  149.7 0.0 copy-start.2
  149.7 215.7 %collective-permute-done.1 = bf16[1,5120,512]{2,1,0:T(8,128)(2,1)} collective-permute-done((bf16[1,5120,512]{2,1,0:T(8,128)(2,1)}, bf16[1,5120,512]{2,1,0:T(8,128)(2,1)}, u32[]{:S(2)}, u32[]{:S(2)}) %collective-permute-start.1) | collective-permute-done | bytes 5242912 | tf_op jit(solution)/shard_map/ppermute | solution.py:25
  365.4 3.8 fusion.2
  369.2 0.0 collective-permute-done.2
  369.2 0.0 copy-done.2
  369.2 5.1 %fusion.5 = f32[3072,512]{1,0:T(8,128)S(1)} fusion(bf16[1,1,3072,512]{3,2,1,0:T(8,128)(2,1)S(1)} %copy-done.2, pred[3072]{0:T(1024)(128)(4,1)S(1)} %iota_compare_fusion, bf16[1,5120,512]{2,1,0:T(8,128)(2,1)} %collective-permute-done.2, bf16[1,5120,512]{2,1,0:T(8,128)(2,1)} %collective-permute-done, bf16[1,5120,512]{2,1,0:T(8,128)(2,1)} %collective-permute-done.1, ...), kind=kOutput, calls=%fused_computation.10 | convolution fusion | flops 1614544896 | bytes 11014656 | tf_op jit(solution)/shard_map/jph,jhk->jpk/dot_general | solution.py:75
  374.3 7.5 %fusion = bf16[1,1,3072,512]{3,2,1,0:T(8,128)(2,1)} fusion(f32[3072,512]{1,0:T(8,128)S(1)} %fusion.5, f32[3072,512]{1,0:T(8,128)S(1)} %fusion.1, f32[3072,512]{1,0:T(8,128)S(1)} %fusion.2, bf16[1,5120,512]{2,1,0:T(8,128)(2,1)} %collective-permute-done.2, f32[]{:T(128)} %bitcast.13, f32[]{:T(128)} %bitcast.10, f32[]{:T(128)} %bitcast.1, ...), kind=kOutput, calls=%fused_computation.2 | convolution fusion | flops 1623195648 | bytes 25694720 | tf_op jit(solution)/shard_map/jph,jhk->jpk/dot_general | solution.py:70
  (4 shorter events, 0.0 us)
Async XLA Ops:
  0.0 4.2 %copy-start = (bf16[1,1,3072,512]{3,2,1,0:T(8,128)(2,1)S(1)}, bf16[1,1,3072,512]{3,2,1,0:T(8,128)(2,1)}, u32[]{:S(2)}) copy-start(bf16[1,1,3072,512]{3,2,1,0:T(8,128)(2,1)} %param.8) | copy-start | bytes 9437188
  0.0 4.2 %copy-start.1 = (bf16[1,1,3072,512]{3,2,1,0:T(8,128)(2,1)S(1)}, bf16[1,1,3072,512]{3,2,1,0:T(8,128)(2,1)}, u32[]{:S(2)}) copy-start(bf16[1,1,3072,512]{3,2,1,0:T(8,128)(2,1)} %param.5) | copy-start | bytes 9437188
  4.2 2.0 copy-start.3
  6.2 138.9 %copy-start.4 = (f32[8,3]{0,1:T(4,128)S(1)}, f32[8,3]{0,1:T(4,128)}, u32[]{:S(2)}) copy-start(f32[8,3]{0,1:T(4,128)} %param.9) | copy-start | bytes 292
  21.3 116.3 %collective-permute-start = (bf16[1,5120,512]{2,1,0:T(8,128)(2,1)}, bf16[1,5120,512]{2,1,0:T(8,128)(2,1)}, u32[]{:S(2)}, u32[]{:S(2)}) collective-permute-start(bf16[1,5120,512]{2,1,0:T(8,128)(2,1)} %pad_maximum_fusion), channel_id=1, source_target_pairs={{0,2},{2,0},{1,3},{3,1},{4,6},{6,4},{5,7},{7,5},{8,10},{10,8},{9,1... | collective-permute-start | bytes 15728648 | tf_op jit(solution)/shard_map/ppermute | solution.py:14
  137.6 227.8 %collective-permute-start.1 = (bf16[1,5120,512]{2,1,0:T(8,128)(2,1)}, bf16[1,5120,512]{2,1,0:T(8,128)(2,1)}, u32[]{:S(2)}, u32[]{:S(2)}) collective-permute-start(bf16[1,5120,512]{2,1,0:T(8,128)(2,1)} %collective-permute-done), channel_id=1, source_target_pairs={{0,4},{4,8},{8,12},{12,16},{16,20},{20,24},{24,28},{1,5},{5,9},{9,... | collective-permute-start | bytes 15728648 | tf_op jit(solution)/shard_map/ppermute | solution.py:25
  143.7 225.5 %collective-permute-start.2 = (bf16[1,5120,512]{2,1,0:T(8,128)(2,1)}, bf16[1,5120,512]{2,1,0:T(8,128)(2,1)}, u32[]{:S(2)}, u32[]{:S(2)}) collective-permute-start(bf16[1,5120,512]{2,1,0:T(8,128)(2,1)} %collective-permute-done), channel_id=1, source_target_pairs={{4,0},{8,4},{12,8},{16,12},{20,16},{24,20},{28,24},{5,1},{9,5},{13... | collective-permute-start | bytes 15728648 | tf_op jit(solution)/shard_map/ppermute | solution.py:27
  149.7 219.5 %copy-start.2 = (bf16[1,1,3072,512]{3,2,1,0:T(8,128)(2,1)S(1)}, bf16[1,1,3072,512]{3,2,1,0:T(8,128)(2,1)}, u32[]{:S(2)}) copy-start(bf16[1,1,3072,512]{3,2,1,0:T(8,128)(2,1)} %param.5) | copy-start | bytes 9437188
where the time goes:
time: 382 us
  waiting for transfers between devices  329 us (86%)
  matrix products  22.1 us (6%)
  other arithmetic  18.5 us (5%)
  starting transfers between devices  10.4 us (3%)
    ppermute x1, waiting for transfers between devices, with_halo(): lax.ppermute(tail, axis, [(i, (i + 1) % count) for i in range(ends)])  216 us
    ppermute x1, waiting for transfers between devices, partner_2(): return lax.ppermute(block, axis, route)  113 us
    concatenate x1, other arithmetic, shards(): jnp.concatenate([masked, hole_coupling[:, 0].reshape(chan_count, 3 * hole...  15.1 us
    dot_general x3, matrix products, shards(): jnp.einsum('jph,jhk->jpk', source[:, :row_count], hole_block, preferred_e...  15 us
  transfers between devices with their start and end apart: 3, of which 2 were waited for; matrix products, arithmetic and copies ran while one was open for 2% of the time, Pallas kernels for 0%

commit v1 on v0

v1 whole, which is shorter than its diff:
```python
import functools

import jax
import jax.numpy as jnp
from jax import lax
from jax.experimental import pallas as pl
from jax.experimental.pallas import tpu as pltpu
from jax.sharding import PartitionSpec as P

MESH = pl.DeviceIdType.MESH
CHUNK = 128
BLOCK = 512
HEAD = 4


def kernel(
    half, chunk, block, head,
    wts, live, amp_hbm, hole_hbm, part_hbm, out_hbm,
    amp, hole, part, acc, inter,
    far_out, far_in, near_out, near_in, side_out, side_in, result,
    amp_sem, part_sem, hole_sem,
    far_s, far_r, near_s, near_r, side_s, side_r, out_s,
):
    rows, holes = amp.shape
    terms = rows // chunk
    mixes = holes // chunk
    total = terms + mixes
    blocks = rows // block

    chan = lax.axis_index("ja")
    label = lax.axis_index("pt")
    pos = lax.rem(chan, half)
    base = chan - pos
    odd = lax.rem(chan, 2)
    near = chan + 1 - 2 * odd
    far_to = base + lax.rem(pos + half - 2 + 4 * odd, half)
    far_from = base + lax.rem(pos + half + 2 - 4 * odd, half)
    side = label + 2 - 4 * lax.rem(lax.div(label, 2), 2)

    def amp_copy(b):
        part_rows = pl.ds(pl.multiple_of(b * block, block), block)
        return pltpu.make_async_copy(amp_hbm.at[0, 0, part_rows], amp.at[part_rows], amp_sem.at[b])

    def part_copy(b):
        part_rows = pl.ds(pl.multiple_of(b * block, block), block)
        return pltpu.make_async_copy(part_hbm.at[0, 0, part_rows], part.at[part_rows], part_sem.at[b])

    hole_copy = pltpu.make_async_copy(hole_hbm.at[0, 0], hole, hole_sem)
    amp_copy(0).start()
    hole_copy.start()
    for b in range(blocks):
        if b:
            amp_copy(b).start()
        part_copy(b).start()

    barrier = pltpu.get_barrier_semaphore()
    targets = [{"ja": near}, {"pt": side}, {"ja": far_to}]
    if half != 4:
        targets.append({"ja": far_from})
    for target in targets:
        pl.semaphore_signal(barrier, inc=1, device_id=target, device_id_type=MESH)

    down = jnp.where(pos > 0, wts[chan, 0], 0.0)
    up = jnp.where(pos < half - 1, wts[chan, 2], 0.0)
    own_w = wts[chan, 1]
    near_slot = 2 - 2 * odd
    far_slot = 2 * odd
    near_w = jnp.where(odd == 0, up, down)
    far_w = jnp.where(odd == 0, down, up)
    live_count = live[0, 0]

    def at(k):
        return pl.ds(pl.multiple_of(k * chunk, chunk), chunk)

    def alive(first, count):
        ids = lax.broadcasted_iota(jnp.int32, (count, holes), 0) + first
        return ids < live_count

    def masked(first, count):
        vals = amp[pl.ds(pl.multiple_of(first, count), count)]
        return jnp.where(alive(first, count), vals, jnp.zeros_like(vals))

    def product(j, slot):
        return jnp.dot(masked(j * chunk, chunk), hole[slot], preferred_element_type=jnp.float32)

    def far_copy(k):
        return pltpu.make_async_remote_copy(
            src_ref=far_out.at[at(k)], dst_ref=far_in.at[at(k)],
            send_sem=far_s.at[k], recv_sem=far_r.at[k],
            device_id={"ja": far_to}, device_id_type=MESH,
        )

    def near_copy(k):
        return pltpu.make_async_remote_copy(
            src_ref=near_out.at[at(k)], dst_ref=near_in.at[at(k)],
            send_sem=near_s.at[k], recv_sem=near_r.at[k],
            device_id={"ja": near}, device_id_type=MESH,
        )

    def side_copy(k):
        return pltpu.make_async_remote_copy(
            src_ref=side_out.at[at(k)], dst_ref=side_in.at[at(k)],
            send_sem=side_s.at[k], recv_sem=side_r.at[k],
            device_id={"pt": side}, device_id_type=MESH,
        )

    def out_copy(j):
        return pltpu.make_async_copy(result.at[at(j)], out_hbm.at[0, 0, at(j)], out_s.at[j])

    def is_mix(k):
        return jnp.logical_and(k >= head, k < head + mixes)

    def fill(k, slot, weight, dst, src):
        def put(value):
            value = weight * value
            if src is not None:
                value = value + src[at(k)].astype(jnp.float32)
            dst[at(k)] = value.astype(jnp.bfloat16)

        @pl.when(is_mix(k))
        def _():
            put(inter[at(jnp.clip(k - head, 0, mixes - 1))].astype(jnp.float32))

        @pl.when(jnp.logical_not(is_mix(k)))
        def _():
            put(product(jnp.where(k < head, k, jnp.maximum(k - mixes, 0)), slot))

    amp_copy(0).wait()
    hole_copy.wait()
    pl.semaphore_wait(barrier, len(targets))

    @pl.loop(0, head)
    def _(k):
        far_out[at(k)] = (far_w * product(k, far_slot)).astype(jnp.bfloat16)
        far_copy(k).start()

    acc[...] = jnp.zeros_like(acc)

    @pl.loop(0, blocks)
    def _(b):
        @pl.when(b > 0)
        def _():
            amp_copy(b).wait()

        part_copy(b).wait()
        first = b * block
        acc[...] += lax.dot_general(
            masked(first, block), part[pl.ds(pl.multiple_of(first, block), block)],
            (((0,), (0,)), ((), ())), preferred_element_type=jnp.float32,
        )

    inter[...] = acc[...].astype(jnp.bfloat16)

    @pl.loop(head, head + mixes)
    def _(k):
        vals = inter[at(k - head)].astype(jnp.float32)
        far_out[at(k)] = (far_w * vals).astype(jnp.bfloat16)
        far_copy(k).start()

    lead = head + mixes
    lag = lead + 2

    @pl.loop(0, lag + terms)
    def _(t):
        @pl.when(t + lead < total)
        def _():
            k = t + lead
            far_out[at(k)] = (far_w * product(k - mixes, far_slot)).astype(jnp.bfloat16)
            far_copy(k).start()

        @pl.when(t < total)
        def _():
            far_copy(t).wait_recv()
            fill(t, near_slot, near_w, near_out, far_in)
            near_copy(t).start()

        @pl.when(jnp.logical_and(t >= 1, t < total + 1))
        def _():
            k = t - 1
            near_copy(k).wait_recv()
            fill(k, 1, own_w, side_out, near_in)
            side_copy(k).start()

        @pl.when(t == lag)
        def _():
            for m in range(mixes):
                side_copy(head + m).wait_recv()

        @pl.when(t >= lag)
        def _():
            j = t - lag
            k = jnp.where(j < head, j, j + mixes)
            side_copy(k).wait_recv()
            mix = side_in[head * chunk : head * chunk + holes]
            value = side_in[at(k)].astype(jnp.float32) + jnp.dot(
                masked(j * chunk, chunk), mix, preferred_element_type=jnp.float32
            )
            value = jnp.where(alive(j * chunk, chunk), value, jnp.zeros_like(value))
            result[at(j)] = value.astype(jnp.bfloat16)
            out_copy(j).start()

    @pl.loop(0, total)
    def _(k):
        far_copy(k).wait_send()
        near_copy(k).wait_send()
        side_copy(k).wait_send()

    @pl.loop(0, terms)
    def _(j):
        out_copy(j).wait()


def shards(half, amplitudes, live_rows, hole_coupling, part_hole, recoupling):
    rows, holes = amplitudes.shape[2:]
    chunk, block = min(CHUNK, holes), min(BLOCK, rows)
    total = (rows + holes) // chunk
    terms = rows // chunk
    bf = jnp.bfloat16
    stream = pltpu.VMEM((rows + holes, holes), bf)
    sems = pltpu.SemaphoreType.DMA
    flops = 10 * rows * holes * holes
    return pl.pallas_call(
        functools.partial(kernel, half, chunk, block, min(HEAD, terms)),
        out_shape=jax.ShapeDtypeStruct(amplitudes.shape, bf),
        in_specs=[pl.BlockSpec(memory_space=pltpu.SMEM)] * 2
        + [pl.BlockSpec(memory_space=pl.ANY)] * 3,
        out_specs=pl.BlockSpec(memory_space=pl.ANY),
        scratch_shapes=[
            pltpu.VMEM((rows, holes), bf),
            pltpu.VMEM((3, holes, holes), bf),
            pltpu.VMEM((rows, holes), bf),
            pltpu.VMEM((holes, holes), jnp.float32),
            pltpu.VMEM((holes, holes), bf),
            stream, stream, stream, stream, stream, stream,
            pltpu.VMEM((rows, holes), bf),
            sems((rows // block,)),
            sems((rows // block,)),
            sems,
            sems((total,)), sems((total,)), sems((total,)),
            sems((total,)), sems((total,)), sems((total,)),
            sems((terms,)),
        ],
        compiler_params=pltpu.CompilerParams(
            collective_id=0, has_side_effects=True, vmem_limit_bytes=56 << 20
        ),
        cost_estimate=pl.CostEstimate(
            flops=flops, bytes_accessed=6 * rows * holes * 2, transcendentals=0
        ),
        name="gt_bar",
    )(recoupling, live_rows, amplitudes, hole_coupling, part_hole)


def solution(mesh):
    in_specs = (
        P("ja", "pt", None, None),
        P("ja", "pt"),
        P("ja", "pt", None, None, None),
        P("ja", "pt", None, None),
        P(),
    )
    out_specs = P("ja", "pt", None, None)
    body = functools.partial(shards, mesh.shape["ja"] // 2)
    return jax.shard_map(body, mesh=mesh, in_specs=in_specs, out_specs=out_specs, check_vma=False)
```

time: 382 us -> 107 us (0.28)
  waiting for transfers between devices: 329 us -> 0 us
  Pallas kernels: 0 us -> 101 us
  matrix products: 22.1 us -> 0 us
  other arithmetic: 18.5 us -> 0 us
  starting transfers between devices: 10.4 us -> 0 us
  local copies, waits for them, and re-layouts: 0.71 us -> 5.1 us
    ppermute x3 -> x0, waiting for transfers between devices: 329 us -> none  [the longest x1 216 us: with_halo(): lax.ppermute(tail, axis, [(i, (i + 1) % count) for i in range(ends)])]
    pallas_call x0 -> x1, Pallas kernels: none -> 101 us  [shards(): pl.pallas_call(functools.partial(kernel, half, chunk, block, min(HEAD, te...]
    dot_general x5 -> x0, matrix products: 22.1 us -> none  [the longest x3 15 us: shards(): jnp.einsum('jph,jhk->jpk', source[:, :row_count], hole_block, preferred_e...]
    concatenate x1 -> x0, other arithmetic: 15.1 us -> none  [shards(): jnp.concatenate([masked, hole_coupling[:, 0].reshape(chan_count, 3 * hole...]
    ppermute x3 -> x0, starting transfers between devices: 10.4 us -> none  [the longest x1 6.02 us: with_halo(): lax.ppermute(tail, axis, [(i, (i + 1) % count) for i in range(ends)])]
    unnamed x10 -> x2, local copies, waits for them, and re-layouts: 0.03 us -> 5.1 us
  transfers between devices with their start and end apart: 3 -> 0, of which waited for: 2 -> 0; matrix products, arithmetic and copies ran while one was open for 2% -> 0% of each run, Pallas kernels for 0% -> 0%
where the time goes in v1:
time: 107 us
  Pallas kernels  101 us (94%)
  local copies, waits for them, and re-layouts  5.1 us (5%)
    pallas_call x1, Pallas kernels, shards(): pl.pallas_call(functools.partial(kernel, half, chunk, block, min(HEAD, te...  101 us
    unnamed x2, local copies, waits for them, and re-layouts  5.1 us

profile of v1, /device:TPU:0, one launch (start us, length us, event | category | flops | bytes accessed | tf_op | source)
XLA Modules:
  0.0 106.8 jit_solution(7118469166632391517)
XLA Ops:
  0.7 1.3 %copy.6.wts = f32[8,3]{1,0:T(8,128)} copy(f32[8,3]{0,1:T(4,128)} %param.9) | data formatting | bytes 192 | tf_op args[4]
  2.0 101.0 %gt_bar.1 = bf16[1,1,3072,512]{3,2,1,0:T(8,128)(2,1)} custom-call(f32[8,3]{1,0:T(8,128)} %copy.6.wts, s32[1,1]{1,0:T(1,128)S(6)} %copy.8.live, bf16[1,1,3072,512]{3,2,1,0:T(8,128)(2,1)} %amp_hbm.1, bf16[1,1,3,512,512]{4,3,2,1,0:T(8,128)(2,1)} %hole_hbm.1, bf16[1,1,3072,512]{3,2,1,0:T(8,128)(2,1)} %part_hbm.1), custom_call_target="tpu_custom_call" | custom-call | flops 8053063680 | bytes 18874368 | tf_op jit(solution)/shard_map/gt_bar/pallas_call | solution.py:222
  103.0 3.8 %copy.9 = bf16[1,1,3072,512]{3,2,1,0:T(8,128)(2,1)} copy(bf16[1,1,3072,512]{3,2,1,0:T(8,128)(2,1)} %gt_bar.1) | data formatting | bytes 6291456

commit v2 on v1

--- a/solution.py
+++ b/solution.py
@@ -11,15 +11,16 @@
 CHUNK = 128
 BLOCK = 512
 HEAD = 4
+GAP = 1
 
 
 def kernel(
     half, chunk, block, head,
-    wts, live, amp_hbm, hole_hbm, part_hbm, out_hbm,
+    wts, live, amp_hbm, hole_hbm, part_hbm, out,
     amp, hole, part, acc, inter,
-    far_out, far_in, near_out, near_in, side_out, side_in, result,
+    far_out, far_in, near_out, near_in, side_out, side_in, near_p, side_p,
     amp_sem, part_sem, hole_sem,
-    far_s, far_r, near_s, near_r, side_s, side_r, out_s,
+    far_s, far_r, near_s, near_r, side_s, side_r,
 ):
     rows, holes = amp.shape
     terms = rows // chunk
@@ -60,9 +61,9 @@
     for target in targets:
         pl.semaphore_signal(barrier, inc=1, device_id=target, device_id_type=MESH)
 
-    down = jnp.where(pos > 0, wts[chan, 0], 0.0)
-    up = jnp.where(pos < half - 1, wts[chan, 2], 0.0)
-    own_w = wts[chan, 1]
+    down = jnp.where(pos > 0, wts[0, chan], 0.0)
+    up = jnp.where(pos < half - 1, wts[2, chan], 0.0)
+    own_w = wts[1, chan]
     near_slot = 2 - 2 * odd
     far_slot = 2 * odd
     near_w = jnp.where(odd == 0, up, down)
@@ -104,26 +105,20 @@
             device_id={"pt": side}, device_id_type=MESH,
         )
 
-    def out_copy(j):
-        return pltpu.make_async_copy(result.at[at(j)], out_hbm.at[0, 0, at(j)], out_s.at[j])
-
     def is_mix(k):
         return jnp.logical_and(k >= head, k < head + mixes)
 
-    def fill(k, slot, weight, dst, src):
-        def put(value):
-            value = weight * value
-            if src is not None:
-                value = value + src[at(k)].astype(jnp.float32)
-            dst[at(k)] = value.astype(jnp.bfloat16)
-
+    def own(k, slot, weight, dst):
         @pl.when(is_mix(k))
         def _():
-            put(inter[at(jnp.clip(k - head, 0, mixes - 1))].astype(jnp.float32))
+            dst[...] = weight * inter[at(jnp.clip(k - head, 0, mixes - 1))].astype(jnp.float32)
 
         @pl.when(jnp.logical_not(is_mix(k)))
         def _():
-            put(product(jnp.where(k < head, k, jnp.maximum(k - mixes, 0)), slot))
+            dst[...] = weight * product(jnp.where(k < head, k, jnp.maximum(k - mixes, 0)), slot)
+
+    def add(k, ready, src, dst):
+        dst[at(k)] = (ready[...] + src[at(k)].astype(jnp.float32)).astype(jnp.bfloat16)
 
     amp_copy(0).wait()
     hole_copy.wait()
@@ -158,7 +153,7 @@
         far_copy(k).start()
 
     lead = head + mixes
-    lag = lead + 2
+    lag = lead + GAP + 2
 
     @pl.loop(0, lag + terms)
     def _(t):
@@ -170,15 +165,23 @@
 
         @pl.when(t < total)
         def _():
+            own(t, near_slot, near_w, near_p)
+
+        @pl.when(jnp.logical_and(t >= GAP, t < total + GAP))
+        def _():
+            own(t - GAP, 1, own_w, side_p)
+
+        @pl.when(t < total)
+        def _():
             far_copy(t).wait_recv()
-            fill(t, near_slot, near_w, near_out, far_in)
+            add(t, near_p, far_in, near_out)
             near_copy(t).start()
 
-        @pl.when(jnp.logical_and(t >= 1, t < total + 1))
-        def _():
-            k = t - 1
+        @pl.when(jnp.logical_and(t >= GAP, t < total + GAP))
+        def _():
+            k = t - GAP
             near_copy(k).wait_recv()
-            fill(k, 1, own_w, side_out, near_in)
+            add(k, side_p, near_in, side_out)
             side_copy(k).start()
 
         @pl.when(t == lag)
@@ -196,18 +199,13 @@
                 masked(j * chunk, chunk), mix, preferred_element_type=jnp.float32
             )
             value = jnp.where(alive(j * chunk, chunk), value, jnp.zeros_like(value))
-            result[at(j)] = value.astype(jnp.bfloat16)
-            out_copy(j).start()
+            out[0, 0, at(j)] = value.astype(jnp.bfloat16)
 
     @pl.loop(0, total)
     def _(k):
         far_copy(k).wait_send()
         near_copy(k).wait_send()
         side_copy(k).wait_send()
-
-    @pl.loop(0, terms)
-    def _(j):
-        out_copy(j).wait()
 
 
 def shards(half, amplitudes, live_rows, hole_coupling, part_hole, recoupling):
@@ -221,10 +219,10 @@
     flops = 10 * rows * holes * holes
     return pl.pallas_call(
         functools.partial(kernel, half, chunk, block, min(HEAD, terms)),
-        out_shape=jax.ShapeDtypeStruct(amplitudes.shape, bf),
+        out_shape=pltpu.VMEM(amplitudes.shape, bf),
         in_specs=[pl.BlockSpec(memory_space=pltpu.SMEM)] * 2
         + [pl.BlockSpec(memory_space=pl.ANY)] * 3,
-        out_specs=pl.BlockSpec(memory_space=pl.ANY),
+        out_specs=pl.BlockSpec(memory_space=pltpu.VMEM),
         scratch_shapes=[
             pltpu.VMEM((rows, holes), bf),
             pltpu.VMEM((3, holes, holes), bf),
@@ -232,22 +230,22 @@
             pltpu.VMEM((holes, holes), jnp.float32),
             pltpu.VMEM((holes, holes), bf),
             stream, stream, stream, stream, stream, stream,
-            pltpu.VMEM((rows, holes), bf),
+            pltpu.VMEM((chunk, holes), jnp.float32),
+            pltpu.VMEM((chunk, holes), jnp.float32),
             sems((rows // block,)),
             sems((rows // block,)),
             sems,
             sems((total,)), sems((total,)), sems((total,)),
             sems((total,)), sems((total,)), sems((total,)),
-            sems((terms,)),
         ],
         compiler_params=pltpu.CompilerParams(
-            collective_id=0, has_side_effects=True, vmem_limit_bytes=56 << 20
+            collective_id=0, has_side_effects=True, vmem_limit_bytes=60 << 20
         ),
         cost_estimate=pl.CostEstimate(
             flops=flops, bytes_accessed=6 * rows * holes * 2, transcendentals=0
         ),
         name="gt_bar",
-    )(recoupling, live_rows, amplitudes, hole_coupling, part_hole)
+    )(recoupling.T, live_rows, amplitudes, hole_coupling, part_hole)
 
 
 def solution(mesh):

time: 107 us -> 102 us (0.953)
  local copies, waits for them, and re-layouts: 5.1 us -> 1.67 us
    unnamed x2 -> x1, local copies, waits for them, and re-layouts: 5.1 us -> 1.67 us
where the time goes in v2:
time: 102 us
  Pallas kernels  100 us (98%)
  local copies, waits for them, and re-layouts  1.67 us (2%)
    pallas_call x1, Pallas kernels, shards(): pl.pallas_call(functools.partial(kernel, half, chunk, block, min(HEAD, te...  100 us

profile of v2, /device:TPU:0, one launch (start us, length us, event | category | flops | bytes accessed | tf_op | source)
XLA Modules:
  0.0 102.3 jit_solution(503615966598314072)
XLA Ops:
  0.7 100.0 %gt_bar.1 = bf16[1,1,3072,512]{3,2,1,0:T(8,128)(2,1)S(1)} custom-call(f32[3,8]{1,0:T(4,128)} %bitcast.1, s32[1,1]{1,0:T(1,128)S(6)} %copy.8.live, bf16[1,1,3072,512]{3,2,1,0:T(8,128)(2,1)} %amp_hbm.1, bf16[1,1,3,512,512]{4,3,2,1,0:T(8,128)(2,1)} %hole_hbm.1, bf16[1,1,3072,512]{3,2,1,0:T(8,128)(2,1)} %part_hbm.1), custom_call_target="tpu_custom_call" | custom-call | flops 8053063680 | bytes 18874368 | tf_op jit(solution)/shard_map/gt_bar/pallas_call | solution.py:220
  100.7 1.7 %copy.7 = bf16[1,1,3072,512]{3,2,1,0:T(8,128)(2,1)} copy(bf16[1,1,3072,512]{3,2,1,0:T(8,128)(2,1)S(1)} %gt_bar.1) | data formatting | bytes 6291456

commit v3 on v2

--- a/solution.py
+++ b/solution.py
@@ -11,22 +11,23 @@
 CHUNK = 128
 BLOCK = 512
 HEAD = 4
-GAP = 1
+GAP = 2
 
 
 def kernel(
     half, chunk, block, head,
     wts, live, amp_hbm, hole_hbm, part_hbm, out,
-    amp, hole, part, acc, inter,
+    amp, hole, part, acc, inter, mix_in, mix, early,
     far_out, far_in, near_out, near_in, side_out, side_in, near_p, side_p,
     amp_sem, part_sem, hole_sem,
-    far_s, far_r, near_s, near_r, side_s, side_r,
+    far_s, far_r, near_s, near_r, side_s, side_r, mix_s, mix_r,
 ):
     rows, holes = amp.shape
     terms = rows // chunk
     mixes = holes // chunk
     total = terms + mixes
     blocks = rows // block
+    split = holes - chunk
 
     chan = lax.axis_index("ja")
     label = lax.axis_index("pt")
@@ -46,13 +47,19 @@
         part_rows = pl.ds(pl.multiple_of(b * block, block), block)
         return pltpu.make_async_copy(part_hbm.at[0, 0, part_rows], part.at[part_rows], part_sem.at[b])
 
-    hole_copy = pltpu.make_async_copy(hole_hbm.at[0, 0], hole, hole_sem)
+    def hole_copy(slot):
+        return pltpu.make_async_copy(hole_hbm.at[0, 0, slot], hole.at[slot], hole_sem.at[slot])
+
+    near_slot = 2 - 2 * odd
+    far_slot = 2 * odd
     amp_copy(0).start()
-    hole_copy.start()
+    hole_copy(far_slot).start()
     for b in range(blocks):
         if b:
             amp_copy(b).start()
         part_copy(b).start()
+    hole_copy(near_slot).start()
+    hole_copy(1).start()
 
     barrier = pltpu.get_barrier_semaphore()
     targets = [{"ja": near}, {"pt": side}, {"ja": far_to}]
@@ -64,8 +71,6 @@
     down = jnp.where(pos > 0, wts[0, chan], 0.0)
     up = jnp.where(pos < half - 1, wts[2, chan], 0.0)
     own_w = wts[1, chan]
-    near_slot = 2 - 2 * odd
-    far_slot = 2 * odd
     near_w = jnp.where(odd == 0, up, down)
     far_w = jnp.where(odd == 0, down, up)
     live_count = live[0, 0]
@@ -105,23 +110,37 @@
             device_id={"pt": side}, device_id_type=MESH,
         )
 
-    def is_mix(k):
-        return jnp.logical_and(k >= head, k < head + mixes)
-
-    def own(k, slot, weight, dst):
-        @pl.when(is_mix(k))
-        def _():
-            dst[...] = weight * inter[at(jnp.clip(k - head, 0, mixes - 1))].astype(jnp.float32)
-
-        @pl.when(jnp.logical_not(is_mix(k)))
-        def _():
-            dst[...] = weight * product(jnp.where(k < head, k, jnp.maximum(k - mixes, 0)), slot)
-
-    def add(k, ready, src, dst):
-        dst[at(k)] = (ready[...] + src[at(k)].astype(jnp.float32)).astype(jnp.bfloat16)
+    def mix_copy(m):
+        return pltpu.make_async_remote_copy(
+            src_ref=inter.at[at(m)], dst_ref=mix_in.at[at(m)],
+            send_sem=mix_s.at[m], recv_sem=mix_r.at[m],
+            device_id={"pt": side}, device_id_type=MESH,
+        )
+
+    def own(k, slot, weight, put):
+        @pl.when(k >= terms)
+        def _():
+            put(weight * mix_in[at(jnp.maximum(k - terms, 0))].astype(jnp.float32))
+
+        @pl.when(k < terms)
+        def _():
+            put(weight * product(jnp.minimum(k, terms - 1), slot))
+
+    def send_far(k):
+        def put(value):
+            far_out[at(k)] = value.astype(jnp.bfloat16)
+
+        own(k, far_slot, far_w, put)
+        far_copy(k).start()
+
+    def put_near(value):
+        near_p[...] = value
+
+    def put_side(value):
+        side_p[...] = value
 
     amp_copy(0).wait()
-    hole_copy.wait()
+    hole_copy(far_slot).wait()
     pl.semaphore_wait(barrier, len(targets))
 
     @pl.loop(0, head)
@@ -146,66 +165,88 @@
 
     inter[...] = acc[...].astype(jnp.bfloat16)
 
-    @pl.loop(head, head + mixes)
-    def _(k):
-        vals = inter[at(k - head)].astype(jnp.float32)
-        far_out[at(k)] = (far_w * vals).astype(jnp.bfloat16)
-        far_copy(k).start()
-
-    lead = head + mixes
-    lag = lead + GAP + 2
-
-    @pl.loop(0, lag + terms)
+    @pl.loop(0, mixes)
+    def _(m):
+        mix_copy(m).start()
+
+    hole_copy(near_slot).wait()
+    hole_copy(1).wait()
+
+    @pl.loop(0, total + GAP)
     def _(t):
-        @pl.when(t + lead < total)
-        def _():
-            k = t + lead
-            far_out[at(k)] = (far_w * product(k - mixes, far_slot)).astype(jnp.bfloat16)
-            far_copy(k).start()
+        @pl.when(t + head == terms)
+        def _():
+            for m in range(mixes):
+                mix_copy(m).wait_recv()
+
+        @pl.when(t + head < total)
+        def _():
+            send_far(t + head)
 
         @pl.when(t < total)
         def _():
-            own(t, near_slot, near_w, near_p)
-
-        @pl.when(jnp.logical_and(t >= GAP, t < total + GAP))
-        def _():
-            own(t - GAP, 1, own_w, side_p)
+            own(t, near_slot, near_w, put_near)
+
+        @pl.when(t >= GAP)
+        def _():
+            own(jnp.maximum(t - GAP, 0), 1, own_w, put_side)
 
         @pl.when(t < total)
         def _():
             far_copy(t).wait_recv()
-            add(t, near_p, far_in, near_out)
+            value = near_p[...] + far_in[at(t)].astype(jnp.float32)
+            near_out[at(t)] = value.astype(jnp.bfloat16)
             near_copy(t).start()
 
-        @pl.when(jnp.logical_and(t >= GAP, t < total + GAP))
-        def _():
-            k = t - GAP
+        @pl.when(t >= GAP)
+        def _():
+            k = jnp.maximum(t - GAP, 0)
             near_copy(k).wait_recv()
-            add(k, side_p, near_in, side_out)
-            side_copy(k).start()
-
-        @pl.when(t == lag)
-        def _():
-            for m in range(mixes):
-                side_copy(head + m).wait_recv()
-
-        @pl.when(t >= lag)
-        def _():
-            j = t - lag
-            k = jnp.where(j < head, j, j + mixes)
-            side_copy(k).wait_recv()
-            mix = side_in[head * chunk : head * chunk + holes]
-            value = side_in[at(k)].astype(jnp.float32) + jnp.dot(
-                masked(j * chunk, chunk), mix, preferred_element_type=jnp.float32
-            )
-            value = jnp.where(alive(j * chunk, chunk), value, jnp.zeros_like(value))
-            out[0, 0, at(j)] = value.astype(jnp.bfloat16)
+            value = (side_p[...] + near_in[at(k)].astype(jnp.float32)).astype(jnp.bfloat16)
+
+            @pl.when(k < terms)
+            def _():
+                j = jnp.minimum(k, terms - 1)
+                side_out[at(j)] = value
+                side_copy(j).start()
+
+            @pl.when(k >= terms)
+            def _():
+                mix[at(jnp.maximum(k - terms, 0))] = value
+
+        @pl.when(t == total + GAP - 2)
+        def _():
+            @pl.loop(0, blocks)
+            def _(b):
+                where = pl.ds(pl.multiple_of(b * block, block), block)
+                early[where] = jnp.dot(
+                    amp[where, :split], mix[:split], preferred_element_type=jnp.float32
+                )
+
+    @pl.loop(0, blocks)
+    def _(b):
+        for c in range(block // chunk):
+            side_copy(b * (block // chunk) + c).wait_recv()
+        where = pl.ds(pl.multiple_of(b * block, block), block)
+        value = early[where] + side_in[where].astype(jnp.float32)
+        value = value + jnp.dot(
+            amp[where, split:], mix[split:], preferred_element_type=jnp.float32
+        )
+        value = jnp.where(alive(b * block, block), value, jnp.zeros_like(value))
+        out[0, 0, where] = value.astype(jnp.bfloat16)
 
     @pl.loop(0, total)
     def _(k):
         far_copy(k).wait_send()
         near_copy(k).wait_send()
+
+    @pl.loop(0, terms)
+    def _(k):
         side_copy(k).wait_send()
+
+    @pl.loop(0, mixes)
+    def _(m):
+        mix_copy(m).wait_send()
 
 
 def shards(half, amplitudes, live_rows, hole_coupling, part_hole, recoupling):
@@ -218,7 +259,7 @@
     sems = pltpu.SemaphoreType.DMA
     flops = 10 * rows * holes * holes
     return pl.pallas_call(
-        functools.partial(kernel, half, chunk, block, min(HEAD, terms)),
+        functools.partial(kernel, half, chunk, block, min(HEAD, block // chunk)),
         out_shape=pltpu.VMEM(amplitudes.shape, bf),
         in_specs=[pl.BlockSpec(memory_space=pltpu.SMEM)] * 2
         + [pl.BlockSpec(memory_space=pl.ANY)] * 3,
@@ -229,14 +270,20 @@
             pltpu.VMEM((rows, holes), bf),
             pltpu.VMEM((holes, holes), jnp.float32),
             pltpu.VMEM((holes, holes), bf),
-            stream, stream, stream, stream, stream, stream,
+            pltpu.VMEM((holes, holes), bf),
+            pltpu.VMEM((holes, holes), bf),
+            pltpu.VMEM((rows, holes), jnp.float32),
+            stream, stream, stream, stream,
+            pltpu.VMEM((rows, holes), bf),
+            pltpu.VMEM((rows, holes), bf),
             pltpu.VMEM((chunk, holes), jnp.float32),
             pltpu.VMEM((chunk, holes), jnp.float32),
             sems((rows // block,)),
             sems((rows // block,)),
-            sems,
-            sems((total,)), sems((total,)), sems((total,)),
-            sems((total,)), sems((total,)), sems((total,)),
+            sems((3,)),
+            sems((total,)), sems((total,)), sems((total,)), sems((total,)),
+            sems((terms,)), sems((terms,)),
+            sems((holes // chunk,)), sems((holes // chunk,)),
         ],
         compiler_params=pltpu.CompilerParams(
             collective_id=0, has_side_effects=True, vmem_limit_bytes=60 << 20

time: 102 us -> 98 us (0.961)
  Pallas kernels: 100 us -> 95.5 us
    pallas_call x1, Pallas kernels: 100 us -> 95.5 us  [shards(): pl.pallas_call(functools.partial(kernel, half, chunk, block, min(HEAD, bl...]
where the time goes in v3:
time: 98 us; the launch traced here: 97.8 us
  Pallas kernels  95.5 us (97%)
  local copies, waits for them, and re-layouts  1.67 us (2%)
    pallas_call x1, Pallas kernels, shards(): pl.pallas_call(functools.partial(kernel, half, chunk, block, min(HEAD, bl...  95.5 us

profile of v3, /device:TPU:0, one launch (start us, length us, event | category | flops | bytes accessed | tf_op | source)
XLA Modules:
  0.0 97.8 jit_solution(91697394445257518)
XLA Ops:
  0.7 95.5 %gt_bar.1 = bf16[1,1,3072,512]{3,2,1,0:T(8,128)(2,1)S(1)} custom-call(f32[3,8]{1,0:T(4,128)} %bitcast.1, s32[1,1]{1,0:T(1,128)S(6)} %copy.8.live, bf16[1,1,3072,512]{3,2,1,0:T(8,128)(2,1)} %amp_hbm.1, bf16[1,1,3,512,512]{4,3,2,1,0:T(8,128)(2,1)} %hole_hbm.1, bf16[1,1,3072,512]{3,2,1,0:T(8,128)(2,1)} %part_hbm.1), custom_call_target="tpu_custom_call" | custom-call | flops 8053063680 | bytes 18874368 | tf_op jit(solution)/shard_map/gt_bar/pallas_call | solution.py:261
  96.1 1.7 %copy.7 = bf16[1,1,3072,512]{3,2,1,0:T(8,128)(2,1)} copy(bf16[1,1,3072,512]{3,2,1,0:T(8,128)(2,1)S(1)} %gt_bar.1) | data formatting | bytes 6291456

commit v4 on v3

--- a/solution.py
+++ b/solution.py
@@ -11,7 +11,7 @@
 CHUNK = 128
 BLOCK = 512
 HEAD = 4
-GAP = 2
+GAP = 3
 
 
 def kernel(

time: 98 us -> 98 us (level)
  no operation moved by 1% of the time
where the time goes in v4:
time: 98 us; the launch traced here: 97.8 us
  Pallas kernels  95.5 us (97%)
  local copies, waits for them, and re-layouts  1.67 us (2%)
    pallas_call x1, Pallas kernels, shards(): pl.pallas_call(functools.partial(kernel, half, chunk, block, min(HEAD, bl...  95.5 us

profile of v4, /device:TPU:0, one launch (start us, length us, event | category | flops | bytes accessed | tf_op | source)
XLA Modules:
  0.0 97.8 jit_solution(5180120280743808107)
XLA Ops:
  0.7 95.5 %gt_bar.1 = bf16[1,1,3072,512]{3,2,1,0:T(8,128)(2,1)S(1)} custom-call(f32[3,8]{1,0:T(4,128)} %bitcast.1, s32[1,1]{1,0:T(1,128)S(6)} %copy.8.live, bf16[1,1,3072,512]{3,2,1,0:T(8,128)(2,1)} %amp_hbm.1, bf16[1,1,3,512,512]{4,3,2,1,0:T(8,128)(2,1)} %hole_hbm.1, bf16[1,1,3072,512]{3,2,1,0:T(8,128)(2,1)} %part_hbm.1), custom_call_target="tpu_custom_call" | custom-call | flops 8053063680 | bytes 18874368 | tf_op jit(solution)/shard_map/gt_bar/pallas_call | solution.py:261
  96.1 1.7 %copy.7 = bf16[1,1,3072,512]{3,2,1,0:T(8,128)(2,1)} copy(bf16[1,1,3072,512]{3,2,1,0:T(8,128)(2,1)S(1)} %gt_bar.1) | data formatting | bytes 6291456
